TPU v7x, 32 devices: a whole 2x2x4 slice. The times are simulated.
32 devices in a mesh: space: 8 (over y, x, core), dp: 4 (over z).
Axes of the slice: x: 2, y: 2, z: 4, core: 2. Of those that a mesh axis runs over, the one named last changes fastest.
Arguments:
- block_in: bfloat16 [4, 8, 56, 56, 128], P('dp', 'space'), may hold values from -6 to 6
- weights: bfloat16 [3, 3, 128, 128], replicated, may hold values from -0.1875 to 0.1875
- out_bias: float32 [128], replicated, may hold values from -3 to 3
- adjacency: int32 [8, 8, 2], P('space'), may hold values from 0 to 7, as said below
- cotangent: bfloat16 [4, 8, 56, 56, 128], P('dp', 'space'), may hold values from -6 to 6
Outputs:
- block_out: bfloat16 [4, 8, 56, 56, 128], P('dp', 'space')
- weight_grad: float32 [3, 3, 128, 128], replicated
- grad_in: bfloat16 [4, 8, 56, 56, 128], P('dp', 'space')
Inputs may be any that keep to these rules, and one draw needn't show every extreme that they name: adjacency[t, e] = (p, f) for e < 4 means that adjacency[p, f] = (t, e): edges are glued in pairs; entries 4 + k hold a tile and corner k' with adjacency[p, 4 + k'] = (t, k), corners glued in pairs. The corner pairing need not follow the edge pairing. Every edge and every corner of every tile appears exactly once as a partner. Column 1 lies in 0..3.
All inputs are finite; a program needn't handle non-finite values.
Results may differ from a plain program's by a relative error of at most 0.0031.
Values may be sent and summed in bfloat16 or wider, within the bound.
A program may use at most 64 MiB of HBM per device.

v0:
```python
import jax
import jax.numpy as jnp
from jax import lax
from jax.sharding import PartitionSpec as P


def tile_edges(field):
    top_rim = field[0, :, :]
    right_rim = field[:, -1, :]
    bottom_rim = jnp.flip(field[-1, :, :], 0)
    left_rim = jnp.flip(field[:, 0, :], 0)
    return jnp.stack([top_rim, right_rim, bottom_rim, left_rim], 0)


def tile_corners(field):
    return jnp.stack([field[0, 0, :], field[0, -1, :], field[-1, -1, :], field[-1, 0, :]], 0)


def assemble(field, near_edges, near_corners):
    top_row = jnp.concatenate([near_corners[0:1], jnp.flip(near_edges[0], 0), near_corners[1:2]], 0)
    bottom_row = jnp.concatenate([near_corners[3:4], near_edges[2], near_corners[2:3]], 0)
    middle = jnp.concatenate(
        [near_edges[3][:, None], field, jnp.flip(near_edges[1], 0)[:, None]], 1
    )
    return jnp.concatenate([top_row[None], middle, bottom_row[None]], 0)


def conv_forward(padded, weights):
    side = padded.shape[0] - 2
    width = padded.shape[2]
    running = jnp.zeros((side * side, weights.shape[3]), jnp.float32)
    for row_off in range(3):
        for col_off in range(3):
            window = padded[row_off : row_off + side, col_off : col_off + side].reshape(
                side * side, width
            )
            running = running + jnp.dot(
                window, weights[row_off, col_off], preferred_element_type=jnp.float32
            )
    return running.reshape(side, side, -1)


def conv_backward(padded, grad_out, weights):
    side = padded.shape[0] - 2
    width = padded.shape[2]
    grad_rows = grad_out.reshape(side * side, -1)
    grad_pad = jnp.zeros(padded.shape, jnp.float32)
    kernel_rows = []
    for row_off in range(3):
        kernel_cols = []
        for col_off in range(3):
            window = padded[row_off : row_off + side, col_off : col_off + side].reshape(
                side * side, width
            )
            kernel_cols.append(jnp.dot(window.T, grad_rows, preferred_element_type=jnp.float32))
            back = jnp.dot(
                grad_rows, weights[row_off, col_off].T, preferred_element_type=jnp.float32
            )
            grad_pad = grad_pad + jnp.pad(
                back.reshape(side, side, width),
                ((row_off, 2 - row_off), (col_off, 2 - col_off), (0, 0)),
            )
        kernel_rows.append(jnp.stack(kernel_cols, 0))
    return (jnp.stack(kernel_rows, 0), grad_pad)


def rim_grads(grad_pad):
    top_rim = grad_pad[0, 1:-1]
    right_rim = grad_pad[1:-1, -1]
    bottom_rim = jnp.flip(grad_pad[-1, 1:-1], 0)
    left_rim = jnp.flip(grad_pad[1:-1, 0], 0)
    rim_edges = jnp.stack([top_rim, right_rim, bottom_rim, left_rim], 0).astype(jnp.bfloat16)
    rim_corners = jnp.stack(
        [grad_pad[0, 0], grad_pad[0, -1], grad_pad[-1, -1], grad_pad[-1, 0]], 0
    ).astype(jnp.bfloat16)
    return (rim_edges, rim_corners)


def add_back(interior, back_edges, back_corners):
    edge_vals = back_edges.astype(jnp.float32)
    corner_vals = back_corners.astype(jnp.float32)
    interior = interior.at[0, :].add(jnp.flip(edge_vals[0], 0))
    interior = interior.at[:, -1].add(jnp.flip(edge_vals[1], 0))
    interior = interior.at[-1, :].add(edge_vals[2])
    interior = interior.at[:, 0].add(edge_vals[3])
    interior = interior.at[0, 0].add(corner_vals[0])
    interior = interior.at[0, -1].add(corner_vals[1])
    interior = interior.at[-1, -1].add(corner_vals[2])
    interior = interior.at[-1, 0].add(corner_vals[3])
    return interior


def glue(edge_cells, corner_cells, link_rows, backward):
    edge_tile = link_rows[0:4, 0]
    edge_side = link_rows[0:4, 1]
    corner_tile = link_rows[4:8, 0]
    corner_side = link_rows[4:8, 1]
    tile_count = lax.axis_size("space")
    tile_ids = jnp.arange(tile_count, dtype=jnp.int32)
    edge_hit = edge_tile[None, :] == tile_ids[:, None]
    corner_hit = corner_tile[None, :] == tile_ids[:, None]
    outgoing = jnp.where(
        edge_hit[:, :, None, None], edge_cells[None], jnp.zeros((), edge_cells.dtype)
    )
    outgoing_corners = jnp.where(
        corner_hit[:, :, None], corner_cells[None], jnp.zeros((), corner_cells.dtype)
    )
    if backward:
        arrived, arrived_corners = (
            lax.all_to_all(outgoing, "space", split_axis=0, concat_axis=0, tiled=True),
            lax.all_to_all(outgoing_corners, "space", split_axis=0, concat_axis=0, tiled=True),
        )
    else:
        arrived, arrived_corners = (
            lax.all_to_all(outgoing, "space", split_axis=0, concat_axis=0, tiled=True),
            lax.all_to_all(outgoing_corners, "space", split_axis=0, concat_axis=0, tiled=True),
        )
    return (arrived[edge_tile, edge_side], arrived_corners[corner_tile, corner_side])


def per_device(block_in, weights, out_bias, adjacency, cotangent):
    inputs = block_in[0, 0]
    link_rows = adjacency[0]
    activation = jax.nn.silu(inputs.astype(jnp.float32)).astype(jnp.bfloat16)
    near_edges, near_corners = glue(
        tile_edges(activation), tile_corners(activation), link_rows, False
    )
    padded = assemble(activation, near_edges, near_corners)
    conv_sum = conv_forward(padded, weights)
    result = (inputs.astype(jnp.float32) + conv_sum + out_bias).astype(jnp.bfloat16)
    grad_out = cotangent[0, 0]
    local_kernel, grad_pad = conv_backward(padded, grad_out, weights)
    rim_edges, rim_corners = rim_grads(grad_pad)
    back_edges, back_corners = glue(rim_edges, rim_corners, link_rows, True)
    act_grad = add_back(grad_pad[1:-1, 1:-1], back_edges, back_corners)
    input_f = inputs.astype(jnp.float32)
    sigmoid_x = jax.nn.sigmoid(input_f)
    grad_in = (
        grad_out.astype(jnp.float32) + act_grad * sigmoid_x * (1.0 + input_f * (1.0 - sigmoid_x))
    ).astype(jnp.bfloat16)
    weight_grad = lax.psum(local_kernel, ("space", "dp"))
    return (result[None, None], weight_grad, grad_in[None, None])


def solution(mesh):
    placed = (
        P("dp", "space", None, None, None),
        P(),
        P(),
        P("space", None, None),
        P("dp", "space", None, None, None),
    )
    return jax.shard_map(
        per_device,
        mesh=mesh,
        in_specs=placed,
        out_specs=(P("dp", "space", None, None, None), P(), P("dp", "space", None, None, None)),
        check_vma=False,
    )
```

profile of v0, /device:TPU:0, one launch (start us, length us, event | category | flops | bytes accessed | tf_op | source)
XLA Modules:
  0.0 241.1 jit_solution(15127318088615724658)
XLA Ops:
  7.2 1.8 fusion.20
  17.5 5.2 %all-to-all-start.3 = ((bf16[8,4,128]{2,1,0:T(4,128)(2,1)}), bf16[8,4,128]{2,1,0:T(4,128)(2,1)}, u32[]{:S(2)}, u32[]{:S(2)}) async-start(bf16[8,4,128]{2,1,0:T(4,128)(2,1)} %broadcast_select_fusion.2), calls=%async_computation.3 | async-start | bytes 16384 | tf_op jit(solution)/shard_map/all_to_all | solution.py:111
  29.2 4.2 %all-to-all-start.2 = ((bf16[8,4,56,128]{3,2,1,0:T(8,128)(2,1)}), bf16[8,4,56,128]{3,2,1,0:T(8,128)(2,1)}, u32[]{:S(2)}, u32[]{:S(2)}) async-start(bf16[8,4,56,128]{3,2,1,0:T(8,128)(2,1)} %broadcast_select_fusion), calls=%async_computation.2 | async-start | bytes 917504 | tf_op jit(solution)/shard_map/all_to_all | solution.py:110
  34.1 1.5 copy.102
  39.3 3.2 %all-to-all-done.2 = bf16[8,4,56,128]{3,2,1,0:T(8,128)(2,1)} async-done(((bf16[8,4,56,128]{3,2,1,0:T(8,128)(2,1)}), bf16[8,4,56,128]{3,2,1,0:T(8,128)(2,1)}, u32[]{:S(2)}, u32[]{:S(2)}) %all-to-all-start.2) | async-done | bytes 458784 | tf_op jit(solution)/shard_map/all_to_all | solution.py:110
  42.5 2.2 gather_fusion.2
  45.6 1.4 slice.479
  47.6 1.4 rev.32
  48.9 1.4 slice_add_fusion.2
  50.3 1.7 scatter-add.26
  54.4 1.8 scatter-add.30
  58.8 2.6 %broadcast_select_fusion.4 = f32[1,1,128]{2,0,1:T(1,128)S(1)} fusion(pred[]{:T(512)} %and_reduce_fusion, f32[56,56,128]{2,0,1:T(8,128)} %scatter-add.34, s32[]{:T(128)} %bitcast.94, s32[]{:T(128)} %bitcast.95, f32[4,128]{1,0:T(4,128)S(1)} %convert_element_type.77), kind=kLoop, calls=%fused_computation.136 | loop fusion | flops 256 | bytes 1545 | tf_op jit(solution)/shard_map/select.13
  61.3 2.5 %scatter-add.35 = f32[56,56,128]{2,0,1:T(8,128)} dynamic-update-slice(f32[56,56,128]{2,0,1:T(8,128)} %scatter-add.34, f32[1,1,128]{2,0,1:T(1,128)S(1)} %broadcast_select_fusion.4, s32[]{:T(128)} %bitcast.94, s32[]{:T(128)} %bitcast.95, s32[]{:T(128)} %constant.227.clone.1) | dynamic-update-slice | bytes 1028 | tf_op jit(solution)/shard_map/scatter-add | solution.py:87
  67.8 2.2 fusion.19
  70.9 3.3 %all-to-all-start = ((bf16[8,4,128]{2,1,0:T(4,128)(2,1)}), bf16[8,4,128]{2,1,0:T(4,128)(2,1)S(1)}, u32[]{:S(2)}, u32[]{:S(2)}) async-start(bf16[8,4,128]{2,1,0:T(4,128)(2,1)} %broadcast_select_fusion.3), calls=%async_computation | async-start | bytes 16384 | tf_op jit(solution)/shard_map/all_to_all | solution.py:116
  75.1 3.7 %all-to-all-done = bf16[8,4,128]{2,1,0:T(4,128)(2,1)S(1)} async-done(((bf16[8,4,128]{2,1,0:T(4,128)(2,1)}), bf16[8,4,128]{2,1,0:T(4,128)(2,1)S(1)}, u32[]{:S(2)}, u32[]{:S(2)}) %all-to-all-start) | async-done | bytes 8224 | tf_op jit(solution)/shard_map/all_to_all | solution.py:116
  78.9 4.1 %all-to-all-start.1 = ((bf16[8,4,56,128]{3,2,1,0:T(8,128)(2,1)}), bf16[8,4,56,128]{3,2,1,0:T(8,128)(2,1)}, u32[]{:S(2)}, u32[]{:S(2)}) async-start(bf16[8,4,56,128]{3,2,1,0:T(8,128)(2,1)} %broadcast_select_fusion.1), calls=%async_computation.1 | async-start | bytes 917504 | tf_op jit(solution)/shard_map/all_to_all | solution.py:115
  83.2 2.2 convolution_bitcast_fusion.4
  87.0 5.1 %all-to-all-done.1 = bf16[8,4,56,128]{3,2,1,0:T(8,128)(2,1)} async-done(((bf16[8,4,56,128]{3,2,1,0:T(8,128)(2,1)}), bf16[8,4,56,128]{3,2,1,0:T(8,128)(2,1)}, u32[]{:S(2)}, u32[]{:S(2)}) %all-to-all-start.1) | async-done | bytes 458784 | tf_op jit(solution)/shard_map/all_to_all | solution.py:115
  92.1 1.6 gather_fusion.1
  95.9 1.5 fusion.46
  105.8 1.8 convolution_add_fusion.7
  115.7 116.7 %all-reduce.11.cloned.1.call-done = f32[3,3,128,128]{3,2,1,0:T(8,128)} async-done(((f32[3,3,128,128]{3,2,1,0:T(8,128)}), f32[3,3,128,128]{3,2,1,0:T(8,128)}) %all-reduce.11.cloned.1.call-update) | async-done | bytes 589840 | tf_op jit(solution)/shard_map/psum | solution.py:141
  232.4 1.9 copy.114
  (156 shorter events, 51.6 us)
Async XLA Ops:
  7.2 1.8 copy-start.14
  7.2 1.8 copy-start
  14.8 1.1 copy-start.24
  15.8 17.6 %copy-start.1 = (bf16[1,1,56,56,128]{4,3,2,1,0:T(8,128)(2,1)S(1)}, bf16[1,1,56,56,128]{4,3,2,1,0:T(8,128)(2,1)}, u32[]{:S(2)}) copy-start(bf16[1,1,56,56,128]{4,3,2,1,0:T(8,128)(2,1)} %param.21) | copy-start | bytes 2408452
  16.8 6.8 %copy-start.22 = (pred[8,4]{1,0:T(8,128)(4,1)}, pred[8,4]{1,0:T(8,128)(4,1)S(1)}, u32[]{:S(2)}) copy-start(pred[8,4]{1,0:T(8,128)(4,1)S(1)} %iota_compare_fusion.1) | copy-start | bytes 100
  17.5 11.7 %all-to-all-start.3 = ((bf16[8,4,128]{2,1,0:T(4,128)(2,1)}), bf16[8,4,128]{2,1,0:T(4,128)(2,1)}, u32[]{:S(2)}, u32[]{:S(2)}) async-start(bf16[8,4,128]{2,1,0:T(4,128)(2,1)} %broadcast_select_fusion.2), calls=%async_computation.3 | async-start | bytes 16384 | tf_op jit(solution)/shard_map/all_to_all | solution.py:111
  27.6 6.5 %copy-start.20 = (pred[8,4]{1,0:T(8,128)(4,1)}, pred[8,4]{1,0:T(8,128)(4,1)S(1)}, u32[]{:S(2)}) copy-start(pred[8,4]{1,0:T(8,128)(4,1)S(1)} %iota_compare_fusion) | copy-start | bytes 100
  29.2 13.3 %all-to-all-start.2 = ((bf16[8,4,56,128]{3,2,1,0:T(8,128)(2,1)}), bf16[8,4,56,128]{3,2,1,0:T(8,128)(2,1)}, u32[]{:S(2)}, u32[]{:S(2)}) async-start(bf16[8,4,56,128]{3,2,1,0:T(8,128)(2,1)} %broadcast_select_fusion), calls=%async_computation.2 | async-start | bytes 917504 | tf_op jit(solution)/shard_map/all_to_all | solution.py:110
  33.8 1.7 copy-start.12
  35.6 1.7 copy-start.25
  35.6 2.4 %copy-start.19 = (s32[4]{0:T(128)S(1)}, s32[4]{0:T(128)}, u32[]{:S(2)}) copy-start(s32[4]{0:T(128)} %get-tuple-element.139) | copy-start | bytes 52
  45.6 1.4 copy-start.17
  67.8 2.4 copy-start.23
  67.8 6.5 %copy-start.21 = (pred[8,4]{1,0:T(8,128)(4,1)S(1)}, pred[8,4]{1,0:T(8,128)(4,1)}, u32[]{:S(2)}) copy-start(pred[8,4]{1,0:T(8,128)(4,1)} %copy-done.20) | copy-start | bytes 100
  70.9 8.0 %all-to-all-start = ((bf16[8,4,128]{2,1,0:T(4,128)(2,1)}), bf16[8,4,128]{2,1,0:T(4,128)(2,1)S(1)}, u32[]{:S(2)}, u32[]{:S(2)}) async-start(bf16[8,4,128]{2,1,0:T(4,128)(2,1)} %broadcast_select_fusion.3), calls=%async_computation | async-start | bytes 16384 | tf_op jit(solution)/shard_map/all_to_all | solution.py:116
  78.9 13.2 %all-to-all-start.1 = ((bf16[8,4,56,128]{3,2,1,0:T(8,128)(2,1)}), bf16[8,4,56,128]{3,2,1,0:T(8,128)(2,1)}, u32[]{:S(2)}, u32[]{:S(2)}) async-start(bf16[8,4,56,128]{3,2,1,0:T(8,128)(2,1)} %broadcast_select_fusion.1), calls=%async_computation.1 | async-start | bytes 917504 | tf_op jit(solution)/shard_map/all_to_all | solution.py:115
  83.0 149.4 %all-reduce.11.cloned.1.call-start = ((), (), s32[]{:S(2)}) async-start(), calls=%async_computation.4 | async-start | bytes 1179648 | tf_op jit(solution)/shard_map/psum | solution.py:141
  103.1 1.4 copy-start.18
  104.5 1.4 copy-start.5
  107.6 1.1 copy-start.7
  108.8 1.1 copy-start.13
  110.2 1.2 copy-start.11
  111.4 1.1 copy-start.9
  112.5 1.1 copy-start.3
  (8 other events, 7.1 us)
Sparse Core Ops, SparseCore 0:
  105.6 126.7 all-reduce.10
where the time goes:
time: 243 us; the launch traced here: 241 us
  waiting for transfers between devices  129 us (53%)
  local copies, waits for them, and re-layouts  42 us (17%)
  other arithmetic  21.2 us (9%)
  matrix products  17.5 us (7%)
  starting transfers between devices  17 us (7%)
  between operations  14.7 us (6%)
    psum x1, waiting for transfers between devices, per_device(): weight_grad = lax.psum(local_kernel, ('space', 'dp'))  117 us
    unnamed x60, local copies, waits for them, and re-layouts  13.6 us
    all_to_all x2, starting transfers between devices, glue(): lax.all_to_all(outgoing_corners, 'space', split_axis=0, concat_axis=0, ti...  8.5 us
    all_to_all x2, starting transfers between devices, glue(): lax.all_to_all(outgoing, 'space', split_axis=0, concat_axis=0, tiled=True)  8.32 us
    all_to_all x2, waiting for transfers between devices, glue(): lax.all_to_all(outgoing, 'space', split_axis=0, concat_axis=0, tiled=True)  8.3 us
    dot_general x9, matrix products, conv_backward(): jnp.dot(grad_rows, weights[row_off, col_off].T, preferred_element_type=jn...  6.31 us
    dot_general x9, matrix products, conv_forward(): jnp.dot(window, weights[row_off, col_off], preferred_element_type=jnp.flo...  5.74 us
    dot_general x9, matrix products, conv_backward(): jnp.dot(window.T, grad_rows, preferred_element_type=jnp.float32)  5.49 us
  transfers between devices with their start and end apart: 5, of which 4 were waited for; matrix products, arithmetic and copies ran while one was open for 9% of the time, Pallas kernels for 0%

commit v1 on v0

--- a/solution.py
+++ b/solution.py
@@ -138,7 +138,7 @@
     grad_in = (
         grad_out.astype(jnp.float32) + act_grad * sigmoid_x * (1.0 + input_f * (1.0 - sigmoid_x))
     ).astype(jnp.bfloat16)
-    weight_grad = lax.psum(local_kernel, ("space", "dp"))
+    weight_grad = lax.psum(lax.psum(local_kernel, "dp"), "space")
     return (result[None, None], weight_grad, grad_in[None, None])
 
 

time: 243 us -> 213 us (0.88)
  waiting for transfers between devices: 129 us -> 98.8 us
    psum x1 -> x2, waiting for transfers between devices: 117 us -> 86.7 us  [per_device(): weight_grad = lax.psum(lax.psum(local_kernel, 'dp'), 'space')]
  transfers between devices with their start and end apart: 5 -> 6, of which waited for: 4 -> 5; matrix products, arithmetic and copies ran while one was open for 9% -> 11% of each run, Pallas kernels for 0% -> 0%
where the time goes in v1:
time: 213 us; the launch traced here: 211 us
  waiting for transfers between devices  98.8 us (46%)
  local copies, waits for them, and re-layouts  41.6 us (20%)
  other arithmetic  21.2 us (10%)
  matrix products  17.5 us (8%)
  starting transfers between devices  17.1 us (8%)
  between operations  14.7 us (7%)
    psum x2, waiting for transfers between devices, per_device(): weight_grad = lax.psum(lax.psum(local_kernel, 'dp'), 'space')  86.7 us
    unnamed x60, local copies, waits for them, and re-layouts  13.2 us
    all_to_all x2, starting transfers between devices, glue(): lax.all_to_all(outgoing_corners, 'space', split_axis=0, concat_axis=0, ti...  8.5 us
    all_to_all x2, starting transfers between devices, glue(): lax.all_to_all(outgoing, 'space', split_axis=0, concat_axis=0, tiled=True)  8.32 us
    all_to_all x2, waiting for transfers between devices, glue(): lax.all_to_all(outgoing, 'space', split_axis=0, concat_axis=0, tiled=True)  8.3 us
    dot_general x9, matrix products, conv_backward(): jnp.dot(grad_rows, weights[row_off, col_off].T, preferred_element_type=jn...  6.31 us
    dot_general x9, matrix products, conv_forward(): jnp.dot(window, weights[row_off, col_off], preferred_element_type=jnp.flo...  5.74 us
    dot_general x9, matrix products, conv_backward(): jnp.dot(window.T, grad_rows, preferred_element_type=jnp.float32)  5.49 us
  transfers between devices with their start and end apart: 6, of which 5 were waited for; matrix products, arithmetic and copies ran while one was open for 11% of the time, Pallas kernels for 0%

profile of v1, /device:TPU:0, one launch (start us, length us, event | category | flops | bytes accessed | tf_op | source)
XLA Modules:
  0.0 210.9 jit_solution(16226935869807019806)
XLA Ops:
  7.2 1.8 fusion.20
  17.5 5.2 %all-to-all-start.3 = ((bf16[8,4,128]{2,1,0:T(4,128)(2,1)}), bf16[8,4,128]{2,1,0:T(4,128)(2,1)}, u32[]{:S(2)}, u32[]{:S(2)}) async-start(bf16[8,4,128]{2,1,0:T(4,128)(2,1)} %broadcast_select_fusion.2), calls=%async_computation.3 | async-start | bytes 16384 | tf_op jit(solution)/shard_map/all_to_all | solution.py:111
  29.2 4.2 %all-to-all-start.2 = ((bf16[8,4,56,128]{3,2,1,0:T(8,128)(2,1)}), bf16[8,4,56,128]{3,2,1,0:T(8,128)(2,1)}, u32[]{:S(2)}, u32[]{:S(2)}) async-start(bf16[8,4,56,128]{3,2,1,0:T(8,128)(2,1)} %broadcast_select_fusion), calls=%async_computation.2 | async-start | bytes 917504 | tf_op jit(solution)/shard_map/all_to_all | solution.py:110
  34.1 1.5 copy.102
  39.3 3.2 %all-to-all-done.2 = bf16[8,4,56,128]{3,2,1,0:T(8,128)(2,1)} async-done(((bf16[8,4,56,128]{3,2,1,0:T(8,128)(2,1)}), bf16[8,4,56,128]{3,2,1,0:T(8,128)(2,1)}, u32[]{:S(2)}, u32[]{:S(2)}) %all-to-all-start.2) | async-done | bytes 458784 | tf_op jit(solution)/shard_map/all_to_all | solution.py:110
  42.5 2.2 %gather_fusion.2 = bf16[4,56,128]{2,1,0:T(8,128)(2,1)} fusion(bf16[8,4,56,128]{3,2,1,0:T(8,128)(2,1)} %all-to-all-done.2, s32[4]{0:T(128)S(1)} %get-tuple-element.140), kind=kCustom, calls=%fused_computation.2 | custom fusion | bytes 114720 | tf_op jit(solution)/shard_map/gather | solution.py:118
  47.6 1.4 rev.32
  48.9 1.4 slice_add_fusion.2
  50.3 1.7 scatter-add.26
  54.4 1.8 scatter-add.30
  58.8 2.6 %broadcast_select_fusion.4 = f32[1,1,128]{2,0,1:T(1,128)S(1)} fusion(pred[]{:T(512)} %and_reduce_fusion, f32[56,56,128]{2,0,1:T(8,128)} %scatter-add.34, s32[]{:T(128)} %bitcast.94, s32[]{:T(128)} %bitcast.95, f32[4,128]{1,0:T(4,128)S(1)} %convert_element_type.77), kind=kLoop, calls=%fused_computation.136 | loop fusion | flops 256 | bytes 1545 | tf_op jit(solution)/shard_map/select.13
  61.3 2.5 %scatter-add.35 = f32[56,56,128]{2,0,1:T(8,128)} dynamic-update-slice(f32[56,56,128]{2,0,1:T(8,128)} %scatter-add.34, f32[1,1,128]{2,0,1:T(1,128)S(1)} %broadcast_select_fusion.4, s32[]{:T(128)} %bitcast.94, s32[]{:T(128)} %bitcast.95, s32[]{:T(128)} %constant.227.clone.1) | dynamic-update-slice | bytes 1028 | tf_op jit(solution)/shard_map/scatter-add | solution.py:87
  67.8 2.2 %fusion.19 = (bf16[1,1,56,56,128]{4,2,3,1,0:T(8,128)(2,1)S(1)}, bf16[56,56,128]{2,0,1:T(8,128)(2,1)S(1)}) fusion(f32[56,56,128]{2,0,1:T(8,128)} %scatter-add.39, bf16[1,1,56,56,128]{4,3,2,1,0:T(8,128)(2,1)S(1)} %copy-done, bf16[1,1,56,56,128]{4,3,2,1,0:T(8,128)(2,1)S(1)} %copy-done.1), kind=kLoop, calls=%fused_computation.49 | loop fusion | flops 5619712 | bytes 4816896 | tf_op jit(solution)/shard_map/broadcast_in_dim | solution.py:142
  70.9 3.3 %all-to-all-start = ((bf16[8,4,128]{2,1,0:T(4,128)(2,1)}), bf16[8,4,128]{2,1,0:T(4,128)(2,1)S(1)}, u32[]{:S(2)}, u32[]{:S(2)}) async-start(bf16[8,4,128]{2,1,0:T(4,128)(2,1)} %broadcast_select_fusion.3), calls=%async_computation | async-start | bytes 16384 | tf_op jit(solution)/shard_map/all_to_all | solution.py:116
  75.1 3.7 %all-to-all-done = bf16[8,4,128]{2,1,0:T(4,128)(2,1)S(1)} async-done(((bf16[8,4,128]{2,1,0:T(4,128)(2,1)}), bf16[8,4,128]{2,1,0:T(4,128)(2,1)S(1)}, u32[]{:S(2)}, u32[]{:S(2)}) %all-to-all-start) | async-done | bytes 8224 | tf_op jit(solution)/shard_map/all_to_all | solution.py:116
  78.9 4.1 %all-to-all-start.1 = ((bf16[8,4,56,128]{3,2,1,0:T(8,128)(2,1)}), bf16[8,4,56,128]{3,2,1,0:T(8,128)(2,1)}, u32[]{:S(2)}, u32[]{:S(2)}) async-start(bf16[8,4,56,128]{3,2,1,0:T(8,128)(2,1)} %broadcast_select_fusion.1), calls=%async_computation.1 | async-start | bytes 917504 | tf_op jit(solution)/shard_map/all_to_all | solution.py:115
  83.2 2.2 %convolution_bitcast_fusion.4 = f32[1,128,128]{2,1,0:T(8,128)} fusion(bf16[56,56,128]{2,1,0:T(8,128)(2,1)S(1)} %bitcast.281, bf16[1,1,56,56,128]{4,2,3,1,0:T(8,128)(2,1)} %copy-done.12), kind=kOutput, calls=%fused_computation.38 | convolution fusion | flops 102760448 | bytes 1671168 | tf_op jit(solution)/shard_map/dot_general | solution.py:55
  87.0 5.1 %all-to-all-done.1 = bf16[8,4,56,128]{3,2,1,0:T(8,128)(2,1)} async-done(((bf16[8,4,56,128]{3,2,1,0:T(8,128)(2,1)}), bf16[8,4,56,128]{3,2,1,0:T(8,128)(2,1)}, u32[]{:S(2)}, u32[]{:S(2)}) %all-to-all-start.1) | async-done | bytes 458784 | tf_op jit(solution)/shard_map/all_to_all | solution.py:115
  92.1 1.6 gather_fusion.1
  95.9 1.5 fusion.46
  105.8 1.8 convolution_add_fusion.7
  114.0 30.4 %all-reduce.12.cloned.1.call-done = f32[3,3,128,128]{3,2,1,0:T(8,128)} async-done(((f32[3,3,128,128]{3,2,1,0:T(8,128)}), f32[3,3,128,128]{3,2,1,0:T(8,128)}) %all-reduce.12.cloned.1.call-update) | async-done | bytes 589840 | tf_op jit(solution)/shard_map/psum | solution.py:141
  145.8 56.4 %all-reduce.14.cloned.1.call-done = f32[3,3,128,128]{3,2,1,0:T(8,128)} async-done(((f32[3,3,128,128]{3,2,1,0:T(8,128)}), f32[3,3,128,128]{3,2,1,0:T(8,128)}) %all-reduce.14.cloned.1.call-update) | async-done | bytes 589840 | tf_op jit(solution)/shard_map/psum | solution.py:141
  202.2 1.9 copy.115
  (159 shorter events, 52.6 us)
Async XLA Ops:
  7.2 1.8 copy-start.14
  7.2 1.8 copy-start
  15.8 17.6 %copy-start.1 = (bf16[1,1,56,56,128]{4,3,2,1,0:T(8,128)(2,1)S(1)}, bf16[1,1,56,56,128]{4,3,2,1,0:T(8,128)(2,1)}, u32[]{:S(2)}) copy-start(bf16[1,1,56,56,128]{4,3,2,1,0:T(8,128)(2,1)} %param.21) | copy-start | bytes 2408452
  16.8 6.8 %copy-start.22 = (pred[8,4]{1,0:T(8,128)(4,1)}, pred[8,4]{1,0:T(8,128)(4,1)S(1)}, u32[]{:S(2)}) copy-start(pred[8,4]{1,0:T(8,128)(4,1)S(1)} %iota_compare_fusion.1) | copy-start | bytes 100
  17.5 11.7 %all-to-all-start.3 = ((bf16[8,4,128]{2,1,0:T(4,128)(2,1)}), bf16[8,4,128]{2,1,0:T(4,128)(2,1)}, u32[]{:S(2)}, u32[]{:S(2)}) async-start(bf16[8,4,128]{2,1,0:T(4,128)(2,1)} %broadcast_select_fusion.2), calls=%async_computation.3 | async-start | bytes 16384 | tf_op jit(solution)/shard_map/all_to_all | solution.py:111
  27.6 6.5 %copy-start.20 = (pred[8,4]{1,0:T(8,128)(4,1)}, pred[8,4]{1,0:T(8,128)(4,1)S(1)}, u32[]{:S(2)}) copy-start(pred[8,4]{1,0:T(8,128)(4,1)S(1)} %iota_compare_fusion) | copy-start | bytes 100
  29.2 13.3 %all-to-all-start.2 = ((bf16[8,4,56,128]{3,2,1,0:T(8,128)(2,1)}), bf16[8,4,56,128]{3,2,1,0:T(8,128)(2,1)}, u32[]{:S(2)}, u32[]{:S(2)}) async-start(bf16[8,4,56,128]{3,2,1,0:T(8,128)(2,1)} %broadcast_select_fusion), calls=%async_computation.2 | async-start | bytes 917504 | tf_op jit(solution)/shard_map/all_to_all | solution.py:110
  33.8 1.7 copy-start.12
  35.6 1.7 copy-start.25
  35.6 2.4 %copy-start.19 = (s32[4]{0:T(128)S(1)}, s32[4]{0:T(128)}, u32[]{:S(2)}) copy-start(s32[4]{0:T(128)} %get-tuple-element.139) | copy-start | bytes 52
  45.6 1.4 copy-start.17
  67.8 2.4 %copy-start.23 = (pred[8,4]{1,0:T(8,128)(4,1)S(1)}, pred[8,4]{1,0:T(8,128)(4,1)}, u32[]{:S(2)}) copy-start(pred[8,4]{1,0:T(8,128)(4,1)} %copy-done.22) | copy-start | bytes 100
  67.8 6.5 %copy-start.21 = (pred[8,4]{1,0:T(8,128)(4,1)S(1)}, pred[8,4]{1,0:T(8,128)(4,1)}, u32[]{:S(2)}) copy-start(pred[8,4]{1,0:T(8,128)(4,1)} %copy-done.20) | copy-start | bytes 100
  70.9 8.0 %all-to-all-start = ((bf16[8,4,128]{2,1,0:T(4,128)(2,1)}), bf16[8,4,128]{2,1,0:T(4,128)(2,1)S(1)}, u32[]{:S(2)}, u32[]{:S(2)}) async-start(bf16[8,4,128]{2,1,0:T(4,128)(2,1)} %broadcast_select_fusion.3), calls=%async_computation | async-start | bytes 16384 | tf_op jit(solution)/shard_map/all_to_all | solution.py:116
  78.9 13.2 %all-to-all-start.1 = ((bf16[8,4,56,128]{3,2,1,0:T(8,128)(2,1)}), bf16[8,4,56,128]{3,2,1,0:T(8,128)(2,1)}, u32[]{:S(2)}, u32[]{:S(2)}) async-start(bf16[8,4,56,128]{3,2,1,0:T(8,128)(2,1)} %broadcast_select_fusion.1), calls=%async_computation.1 | async-start | bytes 917504 | tf_op jit(solution)/shard_map/all_to_all | solution.py:115
  83.0 61.4 %all-reduce.12.cloned.1.call-start = ((), (), s32[]{:S(2)}) async-start(), calls=%async_computation.4 | async-start | bytes 1179648 | tf_op jit(solution)/shard_map/psum | solution.py:141
  103.1 1.4 copy-start.18
  104.5 1.4 copy-start.5
  105.5 96.7 %all-reduce.14.cloned.1.call-start = ((), (), s32[]{:S(2)}) async-start(), calls=%async_computation.5 | async-start | bytes 1179648 | tf_op jit(solution)/shard_map/psum | solution.py:141
  107.6 1.1 copy-start.7
  108.8 1.1 copy-start.13
  110.2 1.1 copy-start.11
  111.4 1.1 copy-start.9
  113.7 30.8 %copy-start.26 = (f32[128]{0:T(128)S(1)}, f32[128]{0:T(128)}, u32[]{:S(2)}) copy-start(f32[128]{0:T(128)} %param.23) | copy-start | bytes 1540
  (9 other events, 8.6 us)
Sparse Core Ops, SparseCore 0:
  105.6 38.7 all-reduce.11
  147.5 54.5 all-reduce.13
